TPU v7x, 512 devices: a whole 4x4x16 slice. The times are simulated.
512 devices in a mesh: grp: 16 (over x, y), mlp: 32 (over z, core).
Axes of the slice: x: 4, y: 4, z: 16, core: 2. Of those that a mesh axis runs over, the one named last changes fastest.
Arguments:
- queries: bfloat16 [65536, 4096], P(('grp', 'mlp')), may hold values from -8 to 8
- keys: bfloat16 [65536, 4096], P(('grp', 'mlp')), may hold values from -8 to 8
- values: bfloat16 [65536, 4096], P(('grp', 'mlp')), may hold values from -6 to 6
- gamma: bfloat16 [4096], P('mlp'), may hold values from 0.25 to 2
- w_merge: bfloat16 [4096, 4096], P('grp', 'mlp'), may hold values from -0.09375 to 0.09375
- grids: int32 [256, 2], P('grp'), may hold values from 8 to 16, as said below
- positions: int32 [16384], replicated, may hold values from 0 to 16383, as said below
Outputs:
- prompt_embeds: bfloat16 [16384, 4096], P('grp', 'mlp')
Inputs may be any that keep to these rules, and one draw needn't show every extreme that they name: `grids`: every grid side is even and at least 8; each group has an image of 16 x 16, and a group's images fill at most 4096 slots. positions is a permutation. From one group's 1024 slots at most 128 go to one block of 1024 consecutive prompt positions, and exactly 128 go to some block.
All inputs are finite; a program needn't handle non-finite values.
Results may differ from a plain program's by a relative error of at most 0.015.
Values may be sent and summed in bfloat16 or wider, within the bound.
No kernel may reach another device: no remote copies, remote signals or barrier semaphores. Data moves between devices by JAX's collectives and lax.ppermute only.
A program may use at most 64 MiB of HBM per device.

v0:
```python
import jax
import jax.numpy as jnp
from jax import lax
from jax.sharding import PartitionSpec as P

HD = 128
GRID = 16


def token_layout(grid, gtok):
    heights = grid[:, 0]
    widths = grid[:, 1]
    areas = heights * widths
    ends = jnp.cumsum(areas)
    starts = ends - areas
    count = grid.shape[0]
    slots = jnp.arange(gtok, dtype=jnp.int32)
    image = jnp.sum((slots[:, None] >= ends[None, :]).astype(jnp.int32), axis=1)
    starts_ext = jnp.concatenate([starts, ends[-1:]])
    widths_ext = jnp.concatenate([widths, jnp.full((1,), 2, jnp.int32)])
    onehot = (image[:, None] == jnp.arange(count + 1, dtype=jnp.int32)[None, :]).astype(jnp.int32)
    first = jnp.sum(onehot * starts_ext[None, :], axis=1)
    width = jnp.sum(onehot * widths_ext[None, :], axis=1)
    local = slots - first
    return (image, local // width, local % width)


def pool_layout(grid, gpool):
    heights = grid[:, 0]
    widths = grid[:, 1]
    areas = heights * widths
    ends = jnp.cumsum(areas)
    starts = ends - areas
    count = grid.shape[0]
    slots = jnp.arange(gpool, dtype=jnp.int32)
    image = jnp.sum((slots[:, None] >= (ends // 4)[None, :]).astype(jnp.int32), axis=1)
    starts_ext = jnp.concatenate([starts, ends[-1:]])
    widths_ext = jnp.concatenate([widths, jnp.full((1,), 2, jnp.int32)])
    onehot = (image[:, None] == jnp.arange(count + 1, dtype=jnp.int32)[None, :]).astype(jnp.int32)
    first = jnp.sum(onehot * starts_ext[None, :], axis=1)
    width = jnp.sum(onehot * widths_ext[None, :], axis=1)
    local = slots - first // 4
    half = width // 2
    anchor = first + 2 * (local // half) * width + 2 * (local % half)
    sources = jnp.stack([anchor, anchor + 1, anchor + width, anchor + width + 1], axis=1)
    sources = jnp.clip(sources, 0, 4 * gpool - 1)
    return (sources, image < count)


def rotate(block, row, col):
    quarter = block.shape[2] // 4
    freq = 100.0 ** (-jnp.arange(quarter, dtype=jnp.float32) / quarter)
    ang_row = row.astype(jnp.float32)[:, None, None] * freq[None, None, :]
    ang_col = col.astype(jnp.float32)[:, None, None] * freq[None, None, :]
    full = block.astype(jnp.float32)
    first = full[..., :quarter]
    second = full[..., quarter : 2 * quarter]
    third = full[..., 2 * quarter : 3 * quarter]
    fourth = full[..., 3 * quarter :]
    out = jnp.concatenate(
        [
            first * jnp.cos(ang_row) - second * jnp.sin(ang_row),
            second * jnp.cos(ang_row) + first * jnp.sin(ang_row),
            third * jnp.cos(ang_col) - fourth * jnp.sin(ang_col),
            fourth * jnp.cos(ang_col) + third * jnp.sin(ang_col),
        ],
        axis=-1,
    )
    return out.astype(jnp.bfloat16)


def attend(rot_q, rot_k, vals, image, qrows, margin):
    gtok = rot_q.shape[0]
    scale = rot_q.shape[2] ** (-0.5)
    pad_k = jnp.pad(rot_k, ((margin, margin), (0, 0), (0, 0)))
    pad_v = jnp.pad(vals, ((margin, margin), (0, 0), (0, 0)))
    pad_id = jnp.pad(image, (margin, margin), constant_values=-1)

    def block(index):
        start = index * qrows
        q_blk = lax.dynamic_slice_in_dim(rot_q, start, qrows, 0)
        k_blk = lax.dynamic_slice_in_dim(pad_k, start, qrows + 2 * margin, 0)
        v_blk = lax.dynamic_slice_in_dim(pad_v, start, qrows + 2 * margin, 0)
        q_ids = lax.dynamic_slice_in_dim(image, start, qrows, 0)
        k_ids = lax.dynamic_slice_in_dim(pad_id, start, qrows + 2 * margin, 0)
        scores = (
            jnp.einsum("qhd,khd->hqk", q_blk, k_blk, preferred_element_type=jnp.float32) * scale
        )
        keep = q_ids[:, None] == k_ids[None, :]
        scores = jnp.where(keep[None, :, :], scores, -1e30)
        top = jnp.max(scores, axis=-1, keepdims=True)
        expo = jnp.exp(scores - top)
        probs = (expo / jnp.sum(expo, axis=-1, keepdims=True)).astype(jnp.bfloat16)
        return jnp.einsum("hqk,khd->qhd", probs, v_blk, preferred_element_type=jnp.float32)

    outs = lax.map(block, jnp.arange(gtok // qrows, dtype=jnp.int32))
    return outs.reshape(gtok, rot_q.shape[1], rot_q.shape[2])


def body(queries, keys, values, gamma, w_merge, grids, positions):
    head_q, head_k, head_v = (
        lax.all_to_all(queries, "mlp", split_axis=1, concat_axis=0, tiled=True),
        lax.all_to_all(keys, "mlp", split_axis=1, concat_axis=0, tiled=True),
        lax.all_to_all(values, "mlp", split_axis=1, concat_axis=0, tiled=True),
    )
    gtok = head_q.shape[0]
    width_dev = head_q.shape[1]
    heads_dev = width_dev // HD
    gpool = gtok // 4
    image, row, col = token_layout(grids, gtok)
    rot_q = rotate(head_q.reshape(gtok, heads_dev, HD), row, col)
    rot_k = rotate(head_k.reshape(gtok, heads_dev, HD), row, col)
    attn = attend(
        rot_q, rot_k, head_v.reshape(gtok, heads_dev, HD), image, min(512, gtok), GRID * GRID
    )
    gains = gamma.astype(jnp.float32).reshape(heads_dev, HD)
    branch = (attn * gains[None, :, :]).astype(jnp.bfloat16).reshape(gtok, width_dev)
    sources, valid = pool_layout(grids, gpool)
    picked = jnp.take(branch, sources, axis=0).astype(jnp.float32)
    pooled = jnp.where(valid[:, None], 0.25 * jnp.sum(picked, axis=1), 0.0).astype(jnp.bfloat16)
    full_columns = lax.all_gather(w_merge, "grp", axis=0, tiled=True)
    merged = jnp.dot(
        lax.all_gather(pooled, "mlp", axis=1, tiled=True),
        full_columns,
        preferred_element_type=jnp.float32,
    ).astype(jnp.bfloat16)
    group = lax.axis_index("grp")
    prompt = positions.shape[0]
    source_of = (
        jnp.zeros((prompt,), jnp.int32).at[positions].set(jnp.arange(prompt, dtype=jnp.int32))
    )
    mine = lax.dynamic_slice_in_dim(source_of, group * gpool, gpool, 0)
    everything = lax.all_gather(merged, "grp", axis=0, tiled=True)
    placed = jnp.take(everything, mine, axis=0)
    return placed


def solution(mesh):
    return jax.shard_map(
        body,
        mesh=mesh,
        in_specs=(
            P(("grp", "mlp"), None),
            P(("grp", "mlp"), None),
            P(("grp", "mlp"), None),
            P("mlp"),
            P("grp", "mlp"),
            P("grp", None),
            P(),
        ),
        out_specs=P("grp", "mlp"),
        check_vma=False,
    )
```

profile of v0, /device:TPU:1, one launch (start us, length us, event | category | flops | bytes accessed | tf_op | source)
XLA Modules:
  0.0 445.1 jit_solution(18084548913521165497)
XLA Ops:
  6.5 2.4 copy.48
  8.9 16.7 %all-to-all-start.1 = ((bf16[128,32,128]{0,2,1:T(8,128)(2,1)}), bf16[128,32,128]{0,2,1:T(8,128)(2,1)S(1)}, u32[]{:S(2)}, u32[]{:S(2)}) async-start(bf16[128,32,128]{0,2,1:T(8,128)(2,1)} %bitcast.15), calls=%async_computation.1 | async-start | bytes 2097152 | tf_op jit(solution)/shard_map/all_to_all | solution.py:102
  27.0 54.4 %all-to-all-done.1 = bf16[128,32,128]{0,2,1:T(8,128)(2,1)S(1)} async-done(((bf16[128,32,128]{0,2,1:T(8,128)(2,1)}), bf16[128,32,128]{0,2,1:T(8,128)(2,1)S(1)}, u32[]{:S(2)}, u32[]{:S(2)}) %all-to-all-start.1) | async-done | bytes 1048608 | tf_op jit(solution)/shard_map/all_to_all | solution.py:102
  81.4 4.1 all-to-all-start.2
  86.9 54.4 %all-to-all-done.2 = bf16[128,32,128]{0,2,1:T(8,128)(2,1)S(1)} async-done(((bf16[128,32,128]{0,2,1:T(8,128)(2,1)}), bf16[128,32,128]{0,2,1:T(8,128)(2,1)S(1)}, u32[]{:S(2)}, u32[]{:S(2)}) %all-to-all-start.2) | async-done | bytes 1048608 | tf_op jit(solution)/shard_map/all_to_all | solution.py:103
  141.3 5.3 %all-to-all-start = ((bf16[128,32,128]{0,2,1:T(8,128)(2,1)}), bf16[128,32,128]{0,2,1:T(8,128)(2,1)}, u32[]{:S(2)}, u32[]{:S(2)}) async-start(bf16[128,32,128]{0,2,1:T(8,128)(2,1)} %bitcast.12), calls=%async_computation | async-start | bytes 2097152 | tf_op jit(solution)/shard_map/all_to_all | solution.py:104
  151.9 2.5 copy.49
  154.4 1.7 reshape.802
  156.4 2.6 copy.51
  158.9 2.7 reshape.803
  161.6 40.8 %all-to-all-done = bf16[128,32,128]{0,2,1:T(8,128)(2,1)} async-done(((bf16[128,32,128]{0,2,1:T(8,128)(2,1)}), bf16[128,32,128]{0,2,1:T(8,128)(2,1)}, u32[]{:S(2)}, u32[]{:S(2)}) %all-to-all-start) | async-done | bytes 1048608 | tf_op jit(solution)/shard_map/all_to_all | solution.py:104
  206.1 4.5 %fusion.31 = (bf16[4096,1,32]{0,2,1:T(8,128)(2,1)S(1)}, bf16[4096,1,32]{0,2,1:T(8,128)(2,1)S(1)}, bf16[4096,1,32]{0,2,1:T(8,128)(2,1)S(1)}, bf16[4096,1,32]{0,2,...) fusion(f32[4096,1,128]{0,2,1:T(8,128)S(1)} %reshape.802, ...), kind=kLoop, calls=%fused_computation.53 | loop fusion | flops 4456448 | bytes 6324352 | tf_op jit(solution)/shard_map/convert.8
  212.8 42.0 %while.10 = (s32[]{:T(128)}, f32[8,512,1,128]{3,1,0,2:T(8,128)S(1)}, s32[8]{0:T(128)S(1)}, bf16[4608,1,128]{2,0,1:T(8,128)(2,1)}, s32[4096]{0:T(1024)S(1)}, /*in...) while((s32[]{:T(128)}, ...), condition=%wide.region_11.12_spmd, body=%wide.region_8.11_spmd.sunk | while | flops 273153024 | bytes 8286440 | solution.py:96
  216.2 1.6 convolution_bitcast_fusion.2
  232.0 1.6 convolution_bitcast_fusion.2
  237.3 1.6 convolution_bitcast_fusion.2
  253.0 1.6 convolution_bitcast_fusion.2
  255.0 12.1 %gather_fusion = bf16[4096,128]{1,0:T(8,128)(2,1)S(1)} fusion(bf16[4096,128]{1,0:T(8,128)(2,1)S(1)} %fusion.10, s32[4096]{0:T(1024)S(1)} %broadcast_clamp_fusion), kind=kCustom, calls=%fused_computation | custom fusion | bytes 2113536 | tf_op jit(solution)/shard_map/jit(_take)/gather | solution.py:119
  267.1 5.8 %convert_reduce_fusion = f32[1024,128]{1,0:T(8,128)S(1)} fusion(bf16[1024,4,128]{2,1,0:T(4,128)(2,1)S(1)} %bitcast.71, pred[1024,4]{1,0:T(8,128)(4,1)S(1)} %copy.45), kind=kLoop, calls=%fused_computation.24 | loop fusion | flops 1441792 | bytes 1576960 | tf_op jit(solution)/shard_map/reduce_sum | solution.py:120
  274.2 88.9 %all-gather.4.cloned.1.call-done = bf16[1024,4096]{1,0:T(8,128)(2,1)} async-done(((bf16[1024,128]{1,0:T(8,128)(2,1)}), bf16[1024,4096]{1,0:T(8,128)(2,1)}) %all-gather.4.cloned.1.call-update) | async-done | bytes 8388624 | tf_op jit(solution)/shard_map/all_gather | solution.py:123
  363.1 6.6 %convolution_convert_fusion = bf16[1024,128]{1,0:T(8,128)(2,1)} fusion(bf16[1024,4096]{1,0:T(8,128)(2,1)} %all-gather.4.cloned.1.call-done, bf16[4096,128]{1,0:T(8,128)(2,1)} %all-gather.6.cloned.1.call-done), kind=kOutput, calls=%fused_computation.25 | convolution fusion | flops 1073872896 | bytes 9699328 | tf_op jit(solution)/shard_map/dot_general | solution.py:122
  369.8 60.3 %scatter_custom_fusion = s32[16384]{0:T(1024)S(1)} fusion(s32[16384]{0:T(1024)S(1)} %compare_select_fusion, s32[16384]{0:T(1024)S(1)} %iota.40, s32[]{:T(128)} %constant.124.clone.1), kind=kCustom, calls=%fused_computation.84 | custom fusion | bytes 65540 | tf_op jit(solution)/shard_map/scatter | solution.py:130
  430.2 1.8 all-gather.8.cloned.1.call-done
  432.0 5.6 %gather_fusion.1 = bf16[1024,128]{1,0:T(8,128)(2,1)S(1)} fusion(bf16[16384,128]{1,0:T(8,128)(2,1)} %all-gather.8.cloned.1.call-done, s32[1024]{0:T(1024)S(1)} %fusion.52), kind=kCustom, calls=%fused_computation.1 | custom fusion | bytes 528384 | tf_op jit(solution)/shard_map/jit(_take)/gather | solution.py:134
  (123 shorter events, 46.8 us)
Async XLA Ops:
  6.5 19.1 %copy-start.2 = (bf16[128,4096]{1,0:T(8,128)(2,1)S(1)}, bf16[128,4096]{1,0:T(8,128)(2,1)}, u32[]{:S(2)}) copy-start(bf16[128,4096]{1,0:T(8,128)(2,1)} %param.10) | copy-start | bytes 3145732
  8.9 72.5 %all-to-all-start.1 = ((bf16[128,32,128]{0,2,1:T(8,128)(2,1)}), bf16[128,32,128]{0,2,1:T(8,128)(2,1)S(1)}, u32[]{:S(2)}, u32[]{:S(2)}) async-start(bf16[128,32,128]{0,2,1:T(8,128)(2,1)} %bitcast.15), calls=%async_computation.1 | async-start | bytes 2097152 | tf_op jit(solution)/shard_map/all_to_all | solution.py:102
  27.0 58.5 %copy-start.3 = (bf16[128,4096]{1,0:T(8,128)(2,1)S(1)}, bf16[128,4096]{1,0:T(8,128)(2,1)}, u32[]{:S(2)}) copy-start(bf16[128,4096]{1,0:T(8,128)(2,1)} %param.11) | copy-start | bytes 3145732
  81.4 59.9 %all-to-all-start.2 = ((bf16[128,32,128]{0,2,1:T(8,128)(2,1)}), bf16[128,32,128]{0,2,1:T(8,128)(2,1)S(1)}, u32[]{:S(2)}, u32[]{:S(2)}) async-start(bf16[128,32,128]{0,2,1:T(8,128)(2,1)} %bitcast.17), calls=%async_computation.2 | async-start | bytes 2097152 | tf_op jit(solution)/shard_map/all_to_all | solution.py:103
  85.5 62.1 %copy-start.5 = (s32[16,2]{0,1:T(2,128)S(1)}, s32[16,2]{0,1:T(2,128)}, u32[]{:S(2)}) copy-start(s32[16,2]{0,1:T(2,128)} %param.14) | copy-start | bytes 388
  85.5 62.8 %copy-start.6 = (bf16[128]{0:T(256)(128)(2,1)S(1)}, bf16[128]{0:T(256)(128)(2,1)}, u32[]{:S(2)}) copy-start(bf16[128]{0:T(256)(128)(2,1)} %param.12) | copy-start | bytes 772
  141.3 61.2 %all-to-all-start = ((bf16[128,32,128]{0,2,1:T(8,128)(2,1)}), bf16[128,32,128]{0,2,1:T(8,128)(2,1)}, u32[]{:S(2)}, u32[]{:S(2)}) async-start(bf16[128,32,128]{0,2,1:T(8,128)(2,1)} %bitcast.12), calls=%async_computation | async-start | bytes 2097152 | tf_op jit(solution)/shard_map/all_to_all | solution.py:104
  146.6 127.6 %all-gather.6.cloned.1.call-start = ((), (), s32[]{:S(2)}) async-start(), calls=%async_computation.4 | async-start | bytes 1114112 | tf_op jit(solution)/shard_map/all_gather | solution.py:121
  147.3 215.8 %all-gather.4.cloned.1.call-start = ((), (), s32[]{:S(2)}) async-start(), calls=%async_computation.3 | async-start | bytes 8650752 | tf_op jit(solution)/shard_map/all_gather | solution.py:123
  204.1 2.0 copy-start
  210.6 2.2 copy-start.1
  273.9 95.9 %copy-start.4 = (s32[16384]{0:T(1024)S(1)}, s32[16384]{0:T(1024)}, u32[]{:S(2)}) copy-start(s32[16384]{0:T(1024)} %param.15) | copy-start | bytes 196612
  273.9 158.1 %all-gather.8.cloned.1.call-start = ((), (), s32[]{:S(2)}) async-start(), calls=%async_computation.5 | async-start | bytes 4456448 | tf_op jit(solution)/shard_map/all_gather | solution.py:133
Sparse Core Ops, SparseCore 0:
  150.4 57.3 all-gather.5
  274.0 89.0 all-gather.3
  369.9 62.0 all-gather.7
where the time goes:
time: 446 us; the launch traced here: 445 us
  waiting for transfers between devices  241 us (54%)
  local copies, waits for them, and re-layouts  105 us (24%)
  matrix products  32.6 us (7%)
  starting transfers between devices  26.6 us (6%)
  other arithmetic  21.6 us (5%)
  between operations  13.4 us (3%)
  loops' own time  4.91 us (1%)
    all_gather x1, waiting for transfers between devices, body(): lax.all_gather(pooled, 'mlp', axis=1, tiled=True)  88.9 us
    scatter x1, local copies, waits for them, and re-layouts, body(): jnp.zeros((prompt,), jnp.int32).at[positions]  60.3 us
    all_to_all x1, waiting for transfers between devices, body(): lax.all_to_all(keys, 'mlp', split_axis=1, concat_axis=0, tiled=True)  54.4 us
    all_to_all x1, waiting for transfers between devices, body(): lax.all_to_all(queries, 'mlp', split_axis=1, concat_axis=0, tiled=True)  54.4 us
    all_to_all x1, waiting for transfers between devices, body(): lax.all_to_all(values, 'mlp', split_axis=1, concat_axis=0, tiled=True)  40.8 us
    all_to_all x1, starting transfers between devices, body(): lax.all_to_all(queries, 'mlp', split_axis=1, concat_axis=0, tiled=True)  16.7 us
    dot_general x8, matrix products, block(): jnp.einsum('hqk,khd->qhd', probs, v_blk, preferred_element_type=jnp.float32)  13.1 us
    dot_general x8, matrix products, block(): jnp.einsum('qhd,khd->hqk', q_blk, k_blk, preferred_element_type=jnp.float32)  12.8 us
  transfers between devices with their start and end apart: 6, of which 5 were waited for; matrix products, arithmetic and copies ran while one was open for 32% of the time, Pallas kernels for 0%

commit v1 on v0

--- a/solution.py
+++ b/solution.py
@@ -120,7 +120,9 @@
     pooled = jnp.where(valid[:, None], 0.25 * jnp.sum(picked, axis=1), 0.0).astype(jnp.bfloat16)
     full_columns = lax.all_gather(w_merge, "grp", axis=0, tiled=True)
     merged = jnp.dot(
-        lax.all_gather(pooled, "mlp", axis=1, tiled=True),
+        jnp.concatenate(
+            lax.all_to_all(jnp.stack([pooled] * lax.axis_size("mlp")), "mlp", 0, 0), axis=1
+        ),
         full_columns,
         preferred_element_type=jnp.float32,
     ).astype(jnp.bfloat16)

time: 446 us -> 734 us (1.65)
  waiting for transfers between devices: 241 us -> 519 us
    all_to_all x0 -> x1, waiting for transfers between devices: none -> 299 us  [body(): lax.all_to_all(jnp.stack([pooled] * lax.axis_size('mlp')), 'mlp', 0, 0)]
    all_gather x1 -> x0, waiting for transfers between devices: 88.9 us -> none  [body(): lax.all_gather(pooled, 'mlp', axis=1, tiled=True)]
    all_gather x1, waiting for transfers between devices: 0.02 us -> 60.6 us  [body(): full_columns = lax.all_gather(w_merge, 'grp', axis=0, tiled=True)]
  transfers between devices with their start and end apart: 6 -> 6, of which waited for: 5 -> 6; matrix products, arithmetic and copies ran while one was open for 32% -> 11% of each run, Pallas kernels for 0% -> 0%
where the time goes in v1:
time: 734 us; the launch traced here: 732 us
  waiting for transfers between devices  519 us (71%)
  local copies, waits for them, and re-layouts  109 us (15%)
  matrix products  32.6 us (4%)
  starting transfers between devices  32 us (4%)
  other arithmetic  20.9 us (3%)
  between operations  13.7 us (2%)
    all_to_all x1, waiting for transfers between devices, body(): lax.all_to_all(jnp.stack([pooled] * lax.axis_size('mlp')), 'mlp', 0, 0)  299 us
    all_gather x1, waiting for transfers between devices, body(): full_columns = lax.all_gather(w_merge, 'grp', axis=0, tiled=True)  60.6 us
    scatter x1, local copies, waits for them, and re-layouts, body(): jnp.zeros((prompt,), jnp.int32).at[positions]  60.3 us
    all_to_all x1, waiting for transfers between devices, body(): lax.all_to_all(keys, 'mlp', split_axis=1, concat_axis=0, tiled=True)  54.4 us
    all_to_all x1, waiting for transfers between devices, body(): lax.all_to_all(queries, 'mlp', split_axis=1, concat_axis=0, tiled=True)  54.4 us
    all_to_all x1, waiting for transfers between devices, body(): lax.all_to_all(values, 'mlp', split_axis=1, concat_axis=0, tiled=True)  41.7 us
    all_to_all x1, starting transfers between devices, body(): lax.all_to_all(queries, 'mlp', split_axis=1, concat_axis=0, tiled=True)  16.7 us
  transfers between devices with their start and end apart: 6, of which 6 were waited for; matrix products, arithmetic and copies ran while one was open for 11% of the time, Pallas kernels for 0%

profile of v1, /device:TPU:1, one launch (start us, length us, event | category | flops | bytes accessed | tf_op | source)
XLA Modules:
  0.0 732.3 jit_solution(5439666161532797573)
XLA Ops:
  6.5 2.4 copy.59
  8.9 16.7 %all-to-all-start.1 = ((bf16[128,32,128]{0,2,1:T(8,128)(2,1)}), bf16[128,32,128]{0,2,1:T(8,128)(2,1)S(1)}, u32[]{:S(2)}, u32[]{:S(2)}) async-start(bf16[128,32,128]{0,2,1:T(8,128)(2,1)} %bitcast.15), calls=%async_computation.1 | async-start | bytes 2097152 | tf_op jit(solution)/shard_map/all_to_all | solution.py:102
  27.0 54.4 %all-to-all-done.1 = bf16[128,32,128]{0,2,1:T(8,128)(2,1)S(1)} async-done(((bf16[128,32,128]{0,2,1:T(8,128)(2,1)}), bf16[128,32,128]{0,2,1:T(8,128)(2,1)S(1)}, u32[]{:S(2)}, u32[]{:S(2)}) %all-to-all-start.1) | async-done | bytes 1048608 | tf_op jit(solution)/shard_map/all_to_all | solution.py:102
  81.4 4.1 all-to-all-start.2
  86.9 54.4 %all-to-all-done.2 = bf16[128,32,128]{0,2,1:T(8,128)(2,1)S(1)} async-done(((bf16[128,32,128]{0,2,1:T(8,128)(2,1)}), bf16[128,32,128]{0,2,1:T(8,128)(2,1)S(1)}, u32[]{:S(2)}, u32[]{:S(2)}) %all-to-all-start.2) | async-done | bytes 1048608 | tf_op jit(solution)/shard_map/all_to_all | solution.py:103
  141.3 5.3 all-to-all-start
  150.9 2.5 copy.60
  153.4 1.7 reshape.818
  155.4 2.6 copy.62
  158.0 2.7 reshape.819
  160.7 41.7 %all-to-all-done = bf16[128,32,128]{0,2,1:T(8,128)(2,1)} async-done(((bf16[128,32,128]{0,2,1:T(8,128)(2,1)}), bf16[128,32,128]{0,2,1:T(8,128)(2,1)}, u32[]{:S(2)}, u32[]{:S(2)}) %all-to-all-start) | async-done | bytes 1048608 | tf_op jit(solution)/shard_map/all_to_all | solution.py:104
  206.1 4.5 fusion.31
  212.8 42.0 %while.10 = (s32[]{:T(128)}, f32[8,512,1,128]{3,1,0,2:T(8,128)S(1)}, s32[8]{0:T(128)S(1)}, bf16[4608,1,128]{2,0,1:T(8,128)(2,1)}, s32[4096]{0:T(1024)S(1)}, /*in...) while((s32[]{:T(128)}, ...), condition=%wide.region_11.12_spmd, body=%wide.region_8.11_spmd.sunk | while | flops 273153024 | bytes 8286440 | solution.py:96
  216.2 1.6 convolution_bitcast_fusion.2
  254.9 12.1 %gather_fusion = bf16[4096,128]{1,0:T(8,128)(2,1)S(1)} fusion(bf16[4096,128]{1,0:T(8,128)(2,1)S(1)} %fusion.10, s32[4096]{0:T(1024)S(1)} %broadcast_clamp_fusion), kind=kCustom, calls=%fused_computation | custom fusion | bytes 2113536 | tf_op jit(solution)/shard_map/jit(_take)/gather | solution.py:119
  267.1 5.8 convert_reduce_fusion
  273.3 4.3 stack.20
  277.6 5.6 all-to-all-start.3
  284.1 60.6 %all-gather.3.cloned.1.call-done = bf16[4096,128]{1,0:T(8,128)(2,1)} async-done(((bf16[256,128]{1,0:T(8,128)(2,1)}), bf16[4096,128]{1,0:T(8,128)(2,1)}) %all-gather.3.cloned.1.call-update) | async-done | bytes 1048592 | tf_op jit(solution)/shard_map/all_gather | solution.py:121
  344.7 298.9 %all-to-all-done.3 = bf16[32,1024,128]{1,2,0:T(8,128)(2,1)} async-done(((bf16[32,1024,128]{1,2,0:T(8,128)(2,1)}), bf16[32,1024,128]{1,2,0:T(8,128)(2,1)}, u32[]{:S(2)}, u32[]{:S(2)}) %all-to-all-start.3) | async-done | bytes 8388640 | tf_op jit(solution)/shard_map/all_to_all | solution.py:124
  643.7 6.7 convolution_convert_fusion
  650.5 60.3 %scatter_custom_fusion = s32[16384]{0:T(1024)S(1)} fusion(s32[16384]{0:T(1024)S(1)} %compare_select_fusion, s32[16384]{0:T(1024)S(1)} %iota.40, s32[]{:T(128)} %constant.124.clone.1), kind=kCustom, calls=%fused_computation.84 | custom fusion | bytes 65540 | tf_op jit(solution)/shard_map/scatter | solution.py:132
  710.9 8.1 %all-gather.5.cloned.1.call-done = bf16[16384,128]{1,0:T(8,128)(2,1)} async-done(((bf16[1024,128]{1,0:T(8,128)(2,1)}), bf16[16384,128]{1,0:T(8,128)(2,1)}) %all-gather.5.cloned.1.call-update) | async-done | bytes 4194320 | tf_op jit(solution)/shard_map/all_gather | solution.py:135
  719.0 5.6 gather_fusion.1
  (124 shorter events, 50.8 us)
Async XLA Ops:
  6.5 19.1 %copy-start.2 = (bf16[128,4096]{1,0:T(8,128)(2,1)S(1)}, bf16[128,4096]{1,0:T(8,128)(2,1)}, u32[]{:S(2)}) copy-start(bf16[128,4096]{1,0:T(8,128)(2,1)} %param.10) | copy-start | bytes 3145732
  8.9 72.5 %all-to-all-start.1 = ((bf16[128,32,128]{0,2,1:T(8,128)(2,1)}), bf16[128,32,128]{0,2,1:T(8,128)(2,1)S(1)}, u32[]{:S(2)}, u32[]{:S(2)}) async-start(bf16[128,32,128]{0,2,1:T(8,128)(2,1)} %bitcast.15), calls=%async_computation.1 | async-start | bytes 2097152 | tf_op jit(solution)/shard_map/all_to_all | solution.py:102
  27.0 58.5 %copy-start.3 = (bf16[128,4096]{1,0:T(8,128)(2,1)S(1)}, bf16[128,4096]{1,0:T(8,128)(2,1)}, u32[]{:S(2)}) copy-start(bf16[128,4096]{1,0:T(8,128)(2,1)} %param.11) | copy-start | bytes 3145732
  81.4 59.9 %all-to-all-start.2 = ((bf16[128,32,128]{0,2,1:T(8,128)(2,1)}), bf16[128,32,128]{0,2,1:T(8,128)(2,1)S(1)}, u32[]{:S(2)}, u32[]{:S(2)}) async-start(bf16[128,32,128]{0,2,1:T(8,128)(2,1)} %bitcast.17), calls=%async_computation.2 | async-start | bytes 2097152 | tf_op jit(solution)/shard_map/all_to_all | solution.py:103
  85.5 61.1 %copy-start.5 = (s32[16,2]{0,1:T(2,128)S(1)}, s32[16,2]{0,1:T(2,128)}, u32[]{:S(2)}) copy-start(s32[16,2]{0,1:T(2,128)} %param.14) | copy-start | bytes 388
  85.5 61.9 %copy-start.6 = (bf16[128]{0:T(256)(128)(2,1)S(1)}, bf16[128]{0:T(256)(128)(2,1)}, u32[]{:S(2)}) copy-start(bf16[128]{0:T(256)(128)(2,1)} %param.12) | copy-start | bytes 772
  141.3 61.2 %all-to-all-start = ((bf16[128,32,128]{0,2,1:T(8,128)(2,1)}), bf16[128,32,128]{0,2,1:T(8,128)(2,1)}, u32[]{:S(2)}, u32[]{:S(2)}) async-start(bf16[128,32,128]{0,2,1:T(8,128)(2,1)} %bitcast.12), calls=%async_computation | async-start | bytes 2097152 | tf_op jit(solution)/shard_map/all_to_all | solution.py:104
  204.1 2.0 copy-start
  210.6 2.2 copy-start.1
  277.6 366.1 %all-to-all-start.3 = ((bf16[32,1024,128]{1,2,0:T(8,128)(2,1)}), bf16[32,1024,128]{1,2,0:T(8,128)(2,1)}, u32[]{:S(2)}, u32[]{:S(2)}) async-start(bf16[32,1024,128]{1,2,0:T(8,128)(2,1)} %stack.20), calls=%async_computation.3 | async-start | bytes 16777216 | tf_op jit(solution)/shard_map/all_to_all | solution.py:124
  283.1 61.6 %all-gather.3.cloned.1.call-start = ((), (), s32[]{:S(2)}) async-start(), calls=%async_computation.4 | async-start | bytes 1114112 | tf_op jit(solution)/shard_map/all_gather | solution.py:121
  283.9 435.1 %all-gather.5.cloned.1.call-start = ((), (), s32[]{:S(2)}) async-start(), calls=%async_computation.5 | async-start | bytes 4456448 | tf_op jit(solution)/shard_map/all_gather | solution.py:135
  643.7 6.8 copy-start.4
Sparse Core Ops, SparseCore 0:
  287.0 57.6 all-gather.2
  650.6 68.3 all-gather.4
